TPU v7x, 256 devices: a whole 4x4x8 slice. The times are simulated.
256 devices in a mesh: layer: 4 (over x), row: 8 (over y, core), col: 8 (over z).
Axes of the slice: x: 4, y: 4, z: 8, core: 2. Of those that a mesh axis runs over, the one named last changes fastest.
Arguments:
- left_values: bfloat16 [8192, 4, 2048], P('row', 'layer', 'col'), may hold values from -22 to 22
- left_pattern: int32 [32, 4, 8], P('row', 'layer', 'col'), may hold values from 0 to 1, as said below
- right_values: bfloat16 [8192, 4, 2048], P(('layer', 'row'), None, 'col'), may hold values from -6 to 6
- right_pattern: int32 [32, 4, 8], P(('layer', 'row'), None, 'col'), may hold values from 0 to 1, as said below
Outputs:
- expanded: bfloat16 [8192, 4, 2048], P('row', 'layer', 'col')
Inputs may be any that keep to these rules, and one draw needn't show every extreme that they name: `left_pattern`: 1 marks a stored tile, 0 an absent one. `right_pattern`: 1 marks a stored tile, 0 an absent one.
All inputs are finite; a program needn't handle non-finite values.
Results may differ from a plain program's by a relative error of at most 0.001.
Values may be sent and summed in bfloat16 or wider, within the bound.
A program may use at most 64 MiB of HBM per device.

v0:
```python
import jax
import jax.numpy as jnp
from jax import lax
from jax.sharding import PartitionSpec as P


def expand_tiles(values, pattern):
    tile_rows, layers, tile_cols = pattern.shape
    tile_size = values.shape[0] // tile_rows
    blocks = values.reshape(tile_rows, tile_size, layers, tile_cols, tile_size)
    blocks = blocks * pattern[:, None, :, :, None].astype(values.dtype)
    return blocks.reshape(values.shape)


def per_device(left_values, left_pattern, right_values, right_pattern):
    left_block = expand_tiles(left_values, left_pattern)
    right_block = expand_tiles(right_values, right_pattern)
    rows_local = left_block.shape[0]
    columns_local = left_block.shape[2]
    left_flat = left_block.reshape(rows_local, columns_local)
    right_rows = lax.all_gather(right_block, "row", axis=0, tiled=True)
    right_mine = lax.all_to_all(right_rows, "layer", split_axis=1, concat_axis=0, tiled=True)
    right_mine = right_mine.reshape(right_mine.shape[0], columns_local)
    product = jnp.dot(
        lax.all_gather(left_flat, ("layer", "col"), axis=1, tiled=True),
        right_mine,
        preferred_element_type=jnp.float32,
    )
    product = product.reshape(rows_local, 1, columns_local)
    squared = product * product
    column = lax.psum(jnp.sum(squared, axis=0, keepdims=True), "row")
    rows_total = rows_local * lax.axis_size("row")
    colmean = column / rows_total
    return (squared / (colmean + 1e-06)).astype(jnp.bfloat16)


def solution(mesh):
    return jax.shard_map(
        per_device,
        mesh=mesh,
        in_specs=(
            P("row", "layer", "col"),
            P("row", "layer", "col"),
            P(("layer", "row"), None, "col"),
            P(("layer", "row"), None, "col"),
        ),
        out_specs=P("row", "layer", "col"),
        check_vma=False,
    )
```

profile of v0, /device:TPU:1, one launch (start us, length us, event | category | flops | bytes accessed | tf_op | source)
XLA Modules:
  0.0 238.1 jit_solution(10458258856644961506)
XLA Ops:
  6.5 0.0 all-gather.5.cloned.1.call-start
  6.5 0.7 convert_bitcast_fusion
  7.2 1.9 copy_multiply_fusion
  9.1 0.0 all-gather.5.cloned.1.call-update
  9.2 0.0 all-gather.3.cloned.1.call-start
  9.2 0.7 convert_bitcast_fusion.1
  9.9 0.1 broadcast_bitcast_fusion
  9.9 2.0 bitcast_multiply_fusion
  12.0 0.0 all-gather.3.cloned.1.call-update
  12.0 36.2 %all-gather.5.cloned.1.call-done = bf16[2048,4,256]{2,0,1:T(8,128)(2,1)} async-done(((bf16[256,4,256]{2,0,1:T(8,128)(2,1)}), bf16[2048,4,256]{2,0,1:T(8,128)(2,1)}) %all-gather.5.cloned.1.call-update) | async-done | bytes 4194320 | tf_op jit(solution)/shard_map/all_gather | solution.py:21
  48.2 62.8 %all_to_all.15 = bf16[2048,4,256]{2,0,1:T(8,128)(2,1)} all-to-all(bf16[2048,4,256]{2,0,1:T(8,128)(2,1)} %all-gather.5.cloned.1.call-done), channel_id=1, replica_groups=mesh['layer'=4,'row'=8,'col'=8] {'layer'}, dimensions={1} | all-to-all | bytes 8388608 | tf_op jit(solution)/shard_map/all_to_all | solution.py:22
  111.0 95.2 %all-gather.3.cloned.1.call-done = bf16[1024,8192]{1,0:T(8,128)(2,1)} async-done(((bf16[1024,256]{1,0:T(8,128)(2,1)}), bf16[1024,8192]{1,0:T(8,128)(2,1)}) %all-gather.3.cloned.1.call-update) | async-done | bytes 16777232 | tf_op jit(solution)/shard_map/all_gather | solution.py:25
  206.1 9.3 %fusion.1 = (f32[256]{0:T(256)S(1)}, f32[1024,256]{1,0:T(8,128)S(1)}) fusion(bf16[1024,8192]{1,0:T(8,128)(2,1)} %all-gather.3.cloned.1.call-done, bf16[8192,256]{1,0:T(8,128)(2,1)} %bitcast.20), kind=kOutput, calls=%fused_computation.9 | convolution fusion | flops 4295491584 | bytes 22021120 | tf_op jit(solution)/shard_map/dot_general | solution.py:24
  215.5 14.9 %psum.7 = f32[1,1,256]{2,1,0:T(1,128)S(1)} all-reduce(f32[1,1,256]{2,1,0:T(1,128)S(1)} %bitcast.23), channel_id=1, replica_groups=mesh['layer'=4,'row'=8,'col'=8] {'row'}, use_global_device_ids=true, to_apply=%region_1.0 | all-reduce | flops 256 | bytes 2048 | tf_op jit(solution)/shard_map/psum | solution.py:31
  230.4 0.9 fusion
  (2 shorter events, 0.0 us)
Async XLA Ops:
  6.5 41.7 %all-gather.5.cloned.1.call-start = ((), (), s32[]{:S(2)}) async-start(), calls=%async_computation.2 | async-start | bytes 4718592 | tf_op jit(solution)/shard_map/all_gather | solution.py:21
  9.2 197.0 %all-gather.3.cloned.1.call-start = ((), (), s32[]{:S(2)}) async-start(), calls=%async_computation.1 | async-start | bytes 17301504 | tf_op jit(solution)/shard_map/all_gather | solution.py:25
Sparse Core Ops, SparseCore 0:
  9.3 38.8 all-gather.4
  50.7 155.4 all-gather.2
where the time goes:
time: 238 us
  waiting for transfers between devices  131 us (55%)
  blocking collectives  77.7 us (33%)
  between operations  13.4 us (6%)
  matrix products  9.32 us (4%)
  other arithmetic  6.17 us (3%)
    all_gather x1, waiting for transfers between devices, per_device(): lax.all_gather(left_flat, ('layer', 'col'), axis=1, tiled=True)  95.2 us
    all_to_all x1, blocking collectives, per_device(): lax.all_to_all(right_rows, 'layer', split_axis=1, concat_axis=0, tiled=True)  62.8 us
    all_gather x1, waiting for transfers between devices, per_device(): right_rows = lax.all_gather(right_block, 'row', axis=0, tiled=True)  36.2 us
    psum x1, blocking collectives, per_device(): column = lax.psum(jnp.sum(squared, axis=0, keepdims=True), 'row')  14.9 us
    dot_general x1, matrix products, per_device(): jnp.dot(lax.all_gather(left_flat, ('layer', 'col'), axis=1, tiled=True),...  9.32 us
  transfers between devices with their start and end apart: 2, of which 2 were waited for; matrix products, arithmetic and copies ran while one was open for 1% of the time, Pallas kernels for 0%

commit v1 on v0

--- a/solution.py
+++ b/solution.py
@@ -28,7 +28,7 @@
     )
     product = product.reshape(rows_local, 1, columns_local)
     squared = product * product
-    column = lax.psum(jnp.sum(squared, axis=0, keepdims=True), "row")
+    column = jnp.sum(lax.all_gather(jnp.sum(squared, axis=0, keepdims=True), "row"), axis=0)
     rows_total = rows_local * lax.axis_size("row")
     colmean = column / rows_total
     return (squared / (colmean + 1e-06)).astype(jnp.bfloat16)

time: 238 us -> 237 us (level)
    psum x1 -> x0, blocking collectives: 14.9 us -> none  [per_device(): column = lax.psum(jnp.sum(squared, axis=0, keepdims=True), 'row')]
    all_gather x0 -> x1, blocking collectives: none -> 13.5 us  [per_device(): lax.all_gather(jnp.sum(squared, axis=0, keepdims=True), 'row')]
where the time goes in v1:
time: 237 us
  waiting for transfers between devices  131 us (55%)
  blocking collectives  76.2 us (32%)
  between operations  13.4 us (6%)
  matrix products  9.32 us (4%)
  other arithmetic  6.2 us (3%)
    all_gather x1, waiting for transfers between devices, per_device(): lax.all_gather(left_flat, ('layer', 'col'), axis=1, tiled=True)  95.2 us
    all_to_all x1, blocking collectives, per_device(): lax.all_to_all(right_rows, 'layer', split_axis=1, concat_axis=0, tiled=True)  62.8 us
    all_gather x1, waiting for transfers between devices, per_device(): right_rows = lax.all_gather(right_block, 'row', axis=0, tiled=True)  36.2 us
    all_gather x1, blocking collectives, per_device(): lax.all_gather(jnp.sum(squared, axis=0, keepdims=True), 'row')  13.5 us
    dot_general x1, matrix products, per_device(): jnp.dot(lax.all_gather(left_flat, ('layer', 'col'), axis=1, tiled=True),...  9.32 us
  transfers between devices with their start and end apart: 2, of which 2 were waited for; matrix products, arithmetic and copies ran while one was open for 1% of the time, Pallas kernels for 0%

profile of v1, /device:TPU:1, one launch (start us, length us, event | category | flops | bytes accessed | tf_op | source)
XLA Modules:
  0.0 236.7 jit_solution(14618837574521213013)
XLA Ops:
  6.5 0.0 all-gather.7.cloned.1.call-start
  6.5 0.7 convert_bitcast_fusion
  7.2 1.9 copy_multiply_fusion
  9.1 0.0 all-gather.7.cloned.1.call-update
  9.2 0.0 all-gather.5.cloned.1.call-start
  9.2 0.7 convert_bitcast_fusion.1
  9.9 0.1 broadcast_bitcast_fusion
  9.9 2.0 bitcast_multiply_fusion
  12.0 0.0 all-gather.5.cloned.1.call-update
  12.0 36.2 %all-gather.7.cloned.1.call-done = bf16[2048,4,256]{2,0,1:T(8,128)(2,1)} async-done(((bf16[256,4,256]{2,0,1:T(8,128)(2,1)}), bf16[2048,4,256]{2,0,1:T(8,128)(2,1)}) %all-gather.7.cloned.1.call-update) | async-done | bytes 4194320 | tf_op jit(solution)/shard_map/all_gather | solution.py:21
  48.2 62.8 %all_to_all.15 = bf16[2048,4,256]{2,0,1:T(8,128)(2,1)} all-to-all(bf16[2048,4,256]{2,0,1:T(8,128)(2,1)} %all-gather.7.cloned.1.call-done), channel_id=1, replica_groups=mesh['layer'=4,'row'=8,'col'=8] {'layer'}, dimensions={1} | all-to-all | bytes 8388608 | tf_op jit(solution)/shard_map/all_to_all | solution.py:22
  111.0 95.2 %all-gather.5.cloned.1.call-done = bf16[1024,8192]{1,0:T(8,128)(2,1)} async-done(((bf16[1024,256]{1,0:T(8,128)(2,1)}), bf16[1024,8192]{1,0:T(8,128)(2,1)}) %all-gather.5.cloned.1.call-update) | async-done | bytes 16777232 | tf_op jit(solution)/shard_map/all_gather | solution.py:25
  206.1 9.3 %fusion.1 = (f32[256]{0:T(256)S(1)}, f32[1024,256]{1,0:T(8,128)S(1)}) fusion(bf16[1024,8192]{1,0:T(8,128)(2,1)} %all-gather.5.cloned.1.call-done, bf16[8192,256]{1,0:T(8,128)(2,1)} %bitcast.19), kind=kOutput, calls=%fused_computation.9 | convolution fusion | flops 4295491584 | bytes 22021120 | tf_op jit(solution)/shard_map/dot_general | solution.py:24
  215.5 13.5 %all-gather.1 = f32[8,1,256]{2,1,0:T(1,128)S(1)} all-gather(f32[1,1,256]{2,1,0:T(1,128)S(1)} %bitcast.21), channel_id=2, replica_groups=mesh['layer'=4,'row'=8,'col'=8] {'row'}, dimensions={0}, use_global_device_ids=true | all-gather | bytes 9216 | tf_op jit(solution)/shard_map/all_gather | solution.py:31
  229.0 0.9 fusion
  (3 shorter events, 0.0 us)
Async XLA Ops:
  6.5 41.7 %all-gather.7.cloned.1.call-start = ((), (), s32[]{:S(2)}) async-start(), calls=%async_computation.2 | async-start | bytes 4718592 | tf_op jit(solution)/shard_map/all_gather | solution.py:21
  9.2 197.0 %all-gather.5.cloned.1.call-start = ((), (), s32[]{:S(2)}) async-start(), calls=%async_computation.1 | async-start | bytes 17301504 | tf_op jit(solution)/shard_map/all_gather | solution.py:25
Sparse Core Ops, SparseCore 0:
  9.3 38.8 all-gather.6
  50.7 155.4 all-gather.4

commit v2 on v0

--- a/solution.py
+++ b/solution.py
@@ -2,6 +2,12 @@
 import jax.numpy as jnp
 from jax import lax
 from jax.sharding import PartitionSpec as P
+
+
+def joined_along(tiles, dim):
+    tiles = jnp.moveaxis(tiles, 0, dim)
+    shape = tiles.shape
+    return tiles.reshape(*shape[:dim], shape[dim] * shape[dim + 1], *shape[dim + 2 :])
 
 
 def expand_tiles(values, pattern):
@@ -18,7 +24,19 @@
     rows_local = left_block.shape[0]
     columns_local = left_block.shape[2]
     left_flat = left_block.reshape(rows_local, columns_local)
-    right_rows = lax.all_gather(right_block, "row", axis=0, tiled=True)
+    size = lax.axis_size("row")
+    pairs = [(i, (i + 1) % size) for i in range(size)]
+    back = [(b, a) for a, b in pairs]
+    lower, upper = ([], [])
+    for step in range(size - 1):
+        if step % 2 == 0:
+            lower.append(lax.ppermute(lower[-1] if lower else right_block, "row", pairs))
+        else:
+            upper.append(lax.ppermute(upper[-1] if upper else right_block, "row", back))
+    tiles = jnp.stack([*lower[::-1], right_block, *upper])
+    shift = lax.axis_index("row") - len(lower)
+    tiles = tiles[(jnp.arange(size) - shift) % size]
+    right_rows = joined_along(tiles, 0)
     right_mine = lax.all_to_all(right_rows, "layer", split_axis=1, concat_axis=0, tiled=True)
     right_mine = right_mine.reshape(right_mine.shape[0], columns_local)
     product = jnp.dot(

time: 238 us -> 238 us (level)
  waiting for transfers between devices: 131 us -> 86.5 us
  local copies, waits for them, and re-layouts: 0.08 us -> 18.5 us
  starting transfers between devices: 0.04 us -> 18 us
  blocking collectives: 77.7 us -> 84.9 us
    all_gather x1 -> x0, waiting for transfers between devices: 36.2 us -> none  [per_device(): right_rows = lax.all_gather(right_block, 'row', axis=0, tiled=True)]
    all_gather x1, waiting for transfers between devices: 95.2 us -> 69.8 us  [per_device(): lax.all_gather(left_flat, ('layer', 'col'), axis=1, tiled=True)]
    ppermute x0 -> x7, starting transfers between devices: none -> 18 us  [the longest x4 10.1 us: per_device(): lax.ppermute(lower[-1] if lower else right_block, 'row', pairs)]
    ppermute x0 -> x7, waiting for transfers between devices: none -> 16.7 us  [the longest x4 15.5 us: per_device(): lax.ppermute(lower[-1] if lower else right_block, 'row', pairs)]
    gather x0 -> x2, local copies, waits for them, and re-layouts: none -> 10.5 us  [per_device(): tiles = tiles[(jnp.arange(size) - shift) % size]]
    all_to_all x1, blocking collectives: 62.8 us -> 71.4 us  [per_device(): lax.all_to_all(right_rows, 'layer', split_axis=1, concat_axis=0, tiled=True)]
    unnamed x2 -> x10, local copies, waits for them, and re-layouts: 0.08 us -> 7 us
  transfers between devices with their start and end apart: 2 -> 8, of which waited for: 2 -> 7; matrix products, arithmetic and copies ran while one was open for 1% -> 9% of each run, Pallas kernels for 0% -> 0%
where the time goes in v2:
time: 238 us; the launch traced here: 237 us
  waiting for transfers between devices  86.5 us (36%)
  blocking collectives  84.9 us (36%)
  local copies, waits for them, and re-layouts  18.5 us (8%)
  starting transfers between devices  18 us (8%)
  between operations  13.4 us (6%)
  matrix products  9.32 us (4%)
  other arithmetic  6.71 us (3%)
    all_to_all x1, blocking collectives, per_device(): lax.all_to_all(right_rows, 'layer', split_axis=1, concat_axis=0, tiled=True)  71.4 us
    all_gather x1, waiting for transfers between devices, per_device(): lax.all_gather(left_flat, ('layer', 'col'), axis=1, tiled=True)  69.8 us
    ppermute x4, waiting for transfers between devices, per_device(): lax.ppermute(lower[-1] if lower else right_block, 'row', pairs)  15.5 us
    psum x1, blocking collectives, per_device(): column = lax.psum(jnp.sum(squared, axis=0, keepdims=True), 'row')  13.5 us
    gather x2, local copies, waits for them, and re-layouts, per_device(): tiles = tiles[(jnp.arange(size) - shift) % size]  10.5 us
    ppermute x4, starting transfers between devices, per_device(): lax.ppermute(lower[-1] if lower else right_block, 'row', pairs)  10.1 us
    dot_general x1, matrix products, per_device(): jnp.dot(lax.all_gather(left_flat, ('layer', 'col'), axis=1, tiled=True),...  9.32 us
    ppermute x3, starting transfers between devices, per_device(): upper.append(lax.ppermute(upper[-1] if upper else right_block, 'row', back))  7.82 us
  transfers between devices with their start and end apart: 8, of which 7 were waited for; matrix products, arithmetic and copies ran while one was open for 9% of the time, Pallas kernels for 0%

profile of v2, /device:TPU:1, one launch (start us, length us, event | category | flops | bytes accessed | tf_op | source)
XLA Modules:
  0.0 237.3 jit_solution(16741400687153011279)
XLA Ops:
  7.3 2.0 bitcast_multiply_fusion
  10.1 1.3 broadcast_multiply_fusion
  11.4 2.7 %collective-permute-start = (bf16[256,4,256]{2,1,0:T(4,128)(2,1)S(1)}, bf16[256,4,256]{2,1,0:T(4,128)(2,1)S(1)}, u32[]{:S(2)}, u32[]{:S(2)}) collective-permute-start(bf16[256,4,256]{2,1,0:T(4,128)(2,1)S(1)} %broadcast_multiply_fusion), channel_id=1, source_target_pairs={{0,8},{8,16},{16,24},{24,32},{32,40},{40,48},{48,56},{56,0},{1,9},... | collective-permute-start | bytes 1572872 | tf_op jit(solution)/shard_map/ppermute | solution.py:33
  14.1 6.1 %collective-permute-done = bf16[256,4,256]{2,1,0:T(4,128)(2,1)S(1)} collective-permute-done((bf16[256,4,256]{2,1,0:T(4,128)(2,1)S(1)}, bf16[256,4,256]{2,1,0:T(4,128)(2,1)S(1)}, u32[]{:S(2)}, u32[]{:S(2)}) %collective-permute-start) | collective-permute-done | bytes 524320 | tf_op jit(solution)/shard_map/ppermute | solution.py:33
  20.2 2.5 %collective-permute-start.1 = (bf16[256,4,256]{2,1,0:T(4,128)(2,1)S(1)}, bf16[256,4,256]{2,1,0:T(4,128)(2,1)S(1)}, u32[]{:S(2)}, u32[]{:S(2)}) collective-permute-start(bf16[256,4,256]{2,1,0:T(4,128)(2,1)S(1)} %collective-permute-done), channel_id=1, source_target_pairs={{0,8},{8,16},{16,24},{24,32},{32,40},{40,48},{48,56},{56,0},{1,9},... | collective-permute-start | bytes 1572872 | tf_op jit(solution)/shard_map/ppermute | solution.py:33
  22.7 1.8 collective-permute-start.4
  24.5 4.4 %collective-permute-done.1 = bf16[256,4,256]{2,1,0:T(4,128)(2,1)S(1)} collective-permute-done((bf16[256,4,256]{2,1,0:T(4,128)(2,1)S(1)}, bf16[256,4,256]{2,1,0:T(4,128)(2,1)S(1)}, u32[]{:S(2)}, u32[]{:S(2)}) %collective-permute-start.1) | collective-permute-done | bytes 524320 | tf_op jit(solution)/shard_map/ppermute | solution.py:33
  28.8 2.5 %collective-permute-start.2 = (bf16[256,4,256]{2,1,0:T(4,128)(2,1)S(1)}, bf16[256,4,256]{2,1,0:T(4,128)(2,1)S(1)}, u32[]{:S(2)}, u32[]{:S(2)}) collective-permute-start(bf16[256,4,256]{2,1,0:T(4,128)(2,1)S(1)} %collective-permute-done.1), channel_id=1, source_target_pairs={{0,8},{8,16},{16,24},{24,32},{32,40},{40,48},{48,56},{56,0},{1,9},... | collective-permute-start | bytes 1572872 | tf_op jit(solution)/shard_map/ppermute | solution.py:33
  31.7 2.6 %collective-permute-start.5 = (bf16[256,4,256]{2,1,0:T(4,128)(2,1)S(1)}, bf16[256,4,256]{2,1,0:T(4,128)(2,1)S(1)}, u32[]{:S(2)}, u32[]{:S(2)}) collective-permute-start(bf16[256,4,256]{2,1,0:T(4,128)(2,1)S(1)} %collective-permute-done.4), channel_id=1, source_target_pairs={{8,0},{16,8},{24,16},{32,24},{40,32},{48,40},{56,48},{0,56},{9,1},... | collective-permute-start | bytes 1572872 | tf_op jit(solution)/shard_map/ppermute | solution.py:35
  34.3 3.1 %collective-permute-done.2 = bf16[256,4,256]{2,1,0:T(4,128)(2,1)S(1)} collective-permute-done((bf16[256,4,256]{2,1,0:T(4,128)(2,1)S(1)}, bf16[256,4,256]{2,1,0:T(4,128)(2,1)S(1)}, u32[]{:S(2)}, u32[]{:S(2)}) %collective-permute-start.2) | collective-permute-done | bytes 524320 | tf_op jit(solution)/shard_map/ppermute | solution.py:33
  37.4 2.5 %collective-permute-start.3 = (bf16[256,4,256]{2,1,0:T(4,128)(2,1)S(1)}, bf16[256,4,256]{2,1,0:T(4,128)(2,1)}, u32[]{:S(2)}, u32[]{:S(2)}) collective-permute-start(bf16[256,4,256]{2,1,0:T(4,128)(2,1)S(1)} %collective-permute-done.2), channel_id=1, source_target_pairs={{0,8},{8,16},{16,24},{24,32},{32,40},{40,48},{48,56},{56,0},{1,9},... | collective-permute-start | bytes 1572872 | tf_op jit(solution)/shard_map/ppermute | solution.py:33
  40.7 3.5 %collective-permute-start.6 = (bf16[256,4,256]{2,1,0:T(4,128)(2,1)S(1)}, bf16[256,4,256]{2,1,0:T(4,128)(2,1)S(1)}, u32[]{:S(2)}, u32[]{:S(2)}) collective-permute-start(bf16[256,4,256]{2,1,0:T(4,128)(2,1)S(1)} %collective-permute-done.5), channel_id=1, source_target_pairs={{8,0},{16,8},{24,16},{32,24},{40,32},{48,40},{56,48},{0,56},{9,1},... | collective-permute-start | bytes 1572872 | tf_op jit(solution)/shard_map/ppermute | solution.py:35
  44.2 1.9 collective-permute-done.3
  46.0 2.0 bitcast_dynamic-update-slice_fusion.7
  49.0 1.0 bitcast_dynamic-update-slice_fusion.5
  50.0 1.0 bitcast_dynamic-update-slice_fusion.4
  51.0 1.1 bitcast_dynamic-update-slice_fusion.3
  52.1 1.0 bitcast_dynamic-update-slice_fusion.2
  55.0 7.6 %gather_fusion = bf16[8,256,4,256]{3,2,1,0:T(4,128)(2,1)} fusion(bf16[8,256,4,256]{3,2,1,0:T(4,128)(2,1)} %bitcast_dynamic-update-slice_fusion, s32[1024]{0:T(1024)S(1)} %pad_clamp_fusion), kind=kCustom, calls=%fused_computation | custom fusion | bytes 8388640 | tf_op jit(solution)/shard_map/gather | solution.py:38
  62.6 2.9 %copy.5 = bf16[8,256,4,256]{3,1,0,2:T(8,128)(2,1)S(1)} copy(bf16[8,256,4,256]{3,2,1,0:T(4,128)(2,1)} %gather_fusion) | data formatting | bytes 8388608 | tf_op jit(solution)/shard_map/gather | solution.py:38
  65.5 71.4 %all_to_all.15 = bf16[2048,4,256]{2,0,1:T(8,128)(2,1)} all-to-all(bf16[2048,4,256]{2,0,1:T(8,128)(2,1)S(1)} %bitcast.39), channel_id=1, replica_groups=mesh['layer'=4,'row'=8,'col'=8] {'layer'}, dimensions={1} | all-to-all | bytes 8388608 | tf_op jit(solution)/shard_map/all_to_all | solution.py:40
  136.9 69.8 %all-gather.2.cloned.1.call-done = bf16[1024,8192]{1,0:T(8,128)(2,1)} async-done(((bf16[1024,256]{1,0:T(8,128)(2,1)}), bf16[1024,8192]{1,0:T(8,128)(2,1)}) %all-gather.2.cloned.1.call-update) | async-done | bytes 16777232 | tf_op jit(solution)/shard_map/all_gather | solution.py:43
  206.7 9.3 %fusion.3 = (f32[256]{0:T(256)S(1)}, f32[1024,256]{1,0:T(8,128)S(1)}) fusion(bf16[1024,8192]{1,0:T(8,128)(2,1)} %all-gather.2.cloned.1.call-done, bf16[8192,256]{1,0:T(8,128)(2,1)} %bitcast.40), kind=kOutput, calls=%fused_computation.25 | convolution fusion | flops 4295491584 | bytes 22021120 | tf_op jit(solution)/shard_map/dot_general | solution.py:42
  216.1 13.5 %psum.7 = f32[1,1,256]{2,1,0:T(1,128)S(1)} all-reduce(f32[1,1,256]{2,1,0:T(1,128)S(1)} %bitcast.43), channel_id=1, replica_groups=mesh['layer'=4,'row'=8,'col'=8] {'row'}, use_global_device_ids=true, to_apply=%region_1.2 | all-reduce | flops 256 | bytes 2048 | tf_op jit(solution)/shard_map/psum | solution.py:49
  (18 shorter events, 6.4 us)
Async XLA Ops:
  6.5 44.5 %copy-start = (bf16[256,4,256]{2,1,0:T(4,128)(2,1)S(1)}, bf16[256,4,256]{2,1,0:T(4,128)(2,1)}, u32[]{:S(2)}) copy-start(bf16[256,4,256]{2,1,0:T(4,128)(2,1)} %param.6) | copy-start | bytes 1572868
  6.5 200.2 %all-gather.2.cloned.1.call-start = ((), (), s32[]{:S(2)}) async-start(), calls=%async_computation.1 | async-start | bytes 17301504 | tf_op jit(solution)/shard_map/all_gather | solution.py:43
  11.4 8.8 %collective-permute-start = (bf16[256,4,256]{2,1,0:T(4,128)(2,1)S(1)}, bf16[256,4,256]{2,1,0:T(4,128)(2,1)S(1)}, u32[]{:S(2)}, u32[]{:S(2)}) collective-permute-start(bf16[256,4,256]{2,1,0:T(4,128)(2,1)S(1)} %broadcast_multiply_fusion), channel_id=1, source_target_pairs={{0,8},{8,16},{16,24},{24,32},{32,40},{40,48},{48,56},{56,0},{1,9},... | collective-permute-start | bytes 1572872 | tf_op jit(solution)/shard_map/ppermute | solution.py:33
  20.2 8.6 %collective-permute-start.1 = (bf16[256,4,256]{2,1,0:T(4,128)(2,1)S(1)}, bf16[256,4,256]{2,1,0:T(4,128)(2,1)S(1)}, u32[]{:S(2)}, u32[]{:S(2)}) collective-permute-start(bf16[256,4,256]{2,1,0:T(4,128)(2,1)S(1)} %collective-permute-done), channel_id=1, source_target_pairs={{0,8},{8,16},{16,24},{24,32},{32,40},{40,48},{48,56},{56,0},{1,9},... | collective-permute-start | bytes 1572872 | tf_op jit(solution)/shard_map/ppermute | solution.py:33
  22.7 9.0 %collective-permute-start.4 = (bf16[256,4,256]{2,1,0:T(4,128)(2,1)S(1)}, bf16[256,4,256]{2,1,0:T(4,128)(2,1)S(1)}, u32[]{:S(2)}, u32[]{:S(2)}) collective-permute-start(bf16[256,4,256]{2,1,0:T(4,128)(2,1)S(1)} %broadcast_multiply_fusion), channel_id=1, source_target_pairs={{8,0},{16,8},{24,16},{32,24},{40,32},{48,40},{56,48},{0,56},{9,1},... | collective-permute-start | bytes 1572872 | tf_op jit(solution)/shard_map/ppermute | solution.py:35
  28.8 8.6 %collective-permute-start.2 = (bf16[256,4,256]{2,1,0:T(4,128)(2,1)S(1)}, bf16[256,4,256]{2,1,0:T(4,128)(2,1)S(1)}, u32[]{:S(2)}, u32[]{:S(2)}) collective-permute-start(bf16[256,4,256]{2,1,0:T(4,128)(2,1)S(1)} %collective-permute-done.1), channel_id=1, source_target_pairs={{0,8},{8,16},{16,24},{24,32},{32,40},{40,48},{48,56},{56,0},{1,9},... | collective-permute-start | bytes 1572872 | tf_op jit(solution)/shard_map/ppermute | solution.py:33
  31.7 9.0 %collective-permute-start.5 = (bf16[256,4,256]{2,1,0:T(4,128)(2,1)S(1)}, bf16[256,4,256]{2,1,0:T(4,128)(2,1)S(1)}, u32[]{:S(2)}, u32[]{:S(2)}) collective-permute-start(bf16[256,4,256]{2,1,0:T(4,128)(2,1)S(1)} %collective-permute-done.4), channel_id=1, source_target_pairs={{8,0},{16,8},{24,16},{32,24},{40,32},{48,40},{56,48},{0,56},{9,1},... | collective-permute-start | bytes 1572872 | tf_op jit(solution)/shard_map/ppermute | solution.py:35
  37.4 8.6 %collective-permute-start.3 = (bf16[256,4,256]{2,1,0:T(4,128)(2,1)S(1)}, bf16[256,4,256]{2,1,0:T(4,128)(2,1)}, u32[]{:S(2)}, u32[]{:S(2)}) collective-permute-start(bf16[256,4,256]{2,1,0:T(4,128)(2,1)S(1)} %collective-permute-done.2), channel_id=1, source_target_pairs={{0,8},{8,16},{16,24},{24,32},{32,40},{40,48},{48,56},{56,0},{1,9},... | collective-permute-start | bytes 1572872 | tf_op jit(solution)/shard_map/ppermute | solution.py:33
  40.7 13.4 %collective-permute-start.6 = (bf16[256,4,256]{2,1,0:T(4,128)(2,1)S(1)}, bf16[256,4,256]{2,1,0:T(4,128)(2,1)S(1)}, u32[]{:S(2)}, u32[]{:S(2)}) collective-permute-start(bf16[256,4,256]{2,1,0:T(4,128)(2,1)S(1)} %collective-permute-done.5), channel_id=1, source_target_pairs={{8,0},{16,8},{24,16},{32,24},{40,32},{48,40},{56,48},{0,56},{9,1},... | collective-permute-start | bytes 1572872 | tf_op jit(solution)/shard_map/ppermute | solution.py:35
Sparse Core Ops, SparseCore 0:
  9.8 196.8 all-gather.1
